TPU v7x, 32 devices: a whole 2x2x4 slice. The times are simulated.
32 devices in a mesh: gx: 2 (over y), gy: 4 (over z), gz: 4 (over x, core).
Axes of the slice: x: 2, y: 2, z: 4, core: 2. Of those that a mesh axis runs over, the one named last changes fastest.
Arguments:
- blocks: float32 [2, 4, 4, 8, 128, 128], P('gx', 'gy', 'gz'), as said below
- columns: int32 [2, 4, 4, 8], replicated, may hold values from -1 to 31, as said below
Outputs:
- purified: float32 [2, 4, 4, 8, 128, 128], P('gx', 'gy', 'gz')
Inputs may be any that keep to these rules, and one draw needn't show every extreme that they name: columns[i, 0] is i itself; every other entry is -1 or the number of a cluster that differs from i by one along exactly one of the three dimensions, repeats allowed. `blocks`: a block in a slot whose column is -1 is zero.
All inputs are finite; a program needn't handle non-finite values.
Results may differ from a plain program's by a relative error of at most 0.0003.
Values sent between devices are 32-bit elements; how exact they have to be, the bound alone decides.
A program may use at most 64 MiB of HBM per device.

v0:
```python
import jax
import jax.numpy as jnp
from jax import lax
from jax.sharding import PartitionSpec as P

exact_mode = lax.Precision.HIGHEST


def shifted(value, axis, steps):
    count = lax.axis_size(axis)
    leading, last = (max(0, -steps), min(count, count - steps))
    return lax.ppermute(value, axis, [(source, source + steps) for source in range(leading, last)])


def extend(current):
    span_x, span_y, span_z = (current.shape[0], current.shape[1], current.shape[2])
    padded = jnp.zeros((span_x + 2, span_y + 2, span_z + 2) + current.shape[3:], jnp.float32)
    padded = padded.at[1 : span_x + 1, 1 : span_y + 1, 1 : span_z + 1].set(current)
    padded = padded.at[0:1, 1 : span_y + 1, 1 : span_z + 1].set(shifted(current, "gx", 1))
    padded = padded.at[span_x + 1 :, 1 : span_y + 1, 1 : span_z + 1].set(shifted(current, "gx", -1))
    padded = padded.at[1 : span_x + 1, 0:1, 1 : span_z + 1].set(shifted(current, "gy", 1))
    padded = padded.at[1 : span_x + 1, span_y + 1 :, 1 : span_z + 1].set(shifted(current, "gy", -1))
    padded = padded.at[1 : span_x + 1, 1 : span_y + 1, 0:1].set(shifted(current, "gz", 1))
    padded = padded.at[1 : span_x + 1, 1 : span_y + 1, span_z + 1 :].set(shifted(current, "gz", -1))
    return padded


def purify(current, slot_index, matches):
    kslots, block_size = (current.shape[3], current.shape[4])
    padded = extend(current).reshape(-1, kslots, block_size, block_size)
    flat_current = current.reshape(-1, kslots, block_size, block_size)
    far_rows = padded[slot_index[0]]
    picked = jnp.einsum("tus,tuab->tsab", matches[0], far_rows, precision=exact_mode)
    row_blocks = flat_current[0]
    square = jnp.einsum("tab,tsbc->sac", row_blocks, picked, precision=exact_mode)
    cubed = jnp.einsum("tab,tsbc->sac", square, picked, precision=exact_mode)
    renewed = 3.0 * square - 2.0 * cubed
    results = [renewed]
    return jnp.stack(results).reshape(current.shape)


def on_device(blocks, columns):
    span_x, span_y, span_z, kslots = (
        blocks.shape[0],
        blocks.shape[1],
        blocks.shape[2],
        blocks.shape[3],
    )
    total_y, total_z = (columns.shape[1], columns.shape[2])
    flat_cols = columns.reshape(-1, kslots)
    base_x = lax.axis_index("gx") * span_x
    base_y = lax.axis_index("gy") * span_y
    base_z = lax.axis_index("gz") * span_z
    own_cols = lax.dynamic_slice(
        columns, (base_x, base_y, base_z, jnp.int32(0)), (span_x, span_y, span_z, kslots)
    ).reshape(-1, kslots)
    safe_cols = jnp.maximum(own_cols, 0)
    pos_x = jnp.clip(safe_cols // (total_y * total_z) - base_x + 1, 0, span_x + 1)
    pos_y = jnp.clip(safe_cols // total_z % total_y - base_y + 1, 0, span_y + 1)
    pos_z = jnp.clip(safe_cols % total_z - base_z + 1, 0, span_z + 1)
    slot_index = (pos_x * (span_y + 2) + pos_y) * (span_z + 2) + pos_z
    far_cols = flat_cols[safe_cols]
    target = own_cols[:, None, None, :]
    matches = (
        (far_cols[:, :, :, None] == target) & (target >= 0) & (own_cols[:, :, None, None] >= 0)
    )
    matches = matches.astype(jnp.float32)
    current = blocks
    current = purify(current, slot_index, matches)
    return current


def solution(mesh):
    return jax.shard_map(
        on_device,
        mesh=mesh,
        in_specs=(P("gx", "gy", "gz", None, None, None), P()),
        out_specs=P("gx", "gy", "gz", None, None, None),
        check_vma=False,
    )
```

profile of v0, /device:TPU:29, one launch (start us, length us, event | category | flops | bytes accessed | tf_op | source)
XLA Modules:
  0.0 69.1 jit_solution(15582256186935587908)
XLA Ops:
  0.0 0.0 copy-start
  0.0 0.0 copy-start.1
  0.0 1.4 %collective-permute-start = (f32[1,1,1,8,128,128]{5,4,3,2,1,0:T(8,128)}, f32[1,1,1,8,128,128]{5,4,3,2,1,0:T(8,128)S(1)}, u32[]{:S(2)}, u32[]{:S(2)}) collective-permute-start(f32[1,1,1,8,128,128]{5,4,3,2,1,0:T(8,128)} %param.16), channel_id=1, source_target_pairs={{0,16},{1,17},{2,18},{3,19},{4,20},{5,21},{6,22},{7,23},{8,24},{9,... | collective-permute-start | bytes 1572872 | tf_op jit(solution)/shard_map/ppermute | solution.py:12
  1.4 4.1 %collective-permute-start.1 = (f32[1,1,1,8,128,128]{5,4,3,2,1,0:T(8,128)}, f32[1,1,1,8,128,128]{5,4,3,2,1,0:T(8,128)S(1)}, u32[]{:S(2)}, u32[]{:S(2)}) collective-permute-start(f32[1,1,1,8,128,128]{5,4,3,2,1,0:T(8,128)} %param.16), channel_id=1, source_target_pairs={{16,0},{17,1},{18,2},{19,3},{20,4},{21,5},{22,6},{23,7},{24,8},{25... | collective-permute-start | bytes 1572872 | tf_op jit(solution)/shard_map/ppermute | solution.py:12
  5.5 1.3 %collective-permute-start.2 = (f32[1,1,1,8,128,128]{5,4,3,2,1,0:T(8,128)}, f32[1,1,1,8,128,128]{5,4,3,2,1,0:T(8,128)S(1)}, u32[]{:S(2)}, u32[]{:S(2)}) collective-permute-start(f32[1,1,1,8,128,128]{5,4,3,2,1,0:T(8,128)} %param.16), channel_id=1, source_target_pairs={{0,4},{4,8},{8,12},{1,5},{5,9},{9,13},{2,6},{6,10},{10,14},{3,7},{... | collective-permute-start | bytes 1572872 | tf_op jit(solution)/shard_map/ppermute | solution.py:12
  6.8 4.0 %collective-permute-start.3 = (f32[1,1,1,8,128,128]{5,4,3,2,1,0:T(8,128)}, f32[1,1,1,8,128,128]{5,4,3,2,1,0:T(8,128)S(1)}, u32[]{:S(2)}, u32[]{:S(2)}) collective-permute-start(f32[1,1,1,8,128,128]{5,4,3,2,1,0:T(8,128)} %param.16), channel_id=1, source_target_pairs={{4,0},{8,4},{12,8},{5,1},{9,5},{13,9},{6,2},{10,6},{14,10},{7,3},{... | collective-permute-start | bytes 1572872 | tf_op jit(solution)/shard_map/ppermute | solution.py:12
  10.8 4.8 %collective-permute-start.4 = (f32[1,1,1,8,128,128]{5,4,3,2,1,0:T(8,128)}, f32[1,1,1,8,128,128]{5,4,3,2,1,0:T(8,128)S(1)}, u32[]{:S(2)}, u32[]{:S(2)}) collective-permute-start(f32[1,1,1,8,128,128]{5,4,3,2,1,0:T(8,128)} %param.16), channel_id=1, source_target_pairs={{0,1},{1,2},{2,3},{4,5},{5,6},{6,7},{8,9},{9,10},{10,11},{12,13},{... | collective-permute-start | bytes 1572872 | tf_op jit(solution)/shard_map/ppermute | solution.py:12
  15.6 0.7 %compare_bitcast_fusion = (pred[8]{0:T(512)(128)(4,1)S(1)}, s32[1,1,1,8]{3,2,1,0:T(1,128)S(1)}) fusion(s32[2,4,4,8]{3,2,1,0:T(4,128)} %param.17, s32[]{:T(128)S(6)} %select_n.79, s32[]{:T(128)S(6)} %select_n.80, s32[]{:T(128)S(6)} %select_n.81), kind=kLoop, calls=%fused_computation.32 | loop fusion | flops 8 | bytes 84 | tf_op jit(solution)/shard_map/and | solution.py:65
  16.4 7.9 %scatter.24 = f32[3,3,3,8,128,128]{5,4,3,2,1,0:T(8,128)} pad(f32[1,1,1,8,128,128]{5,4,3,2,1,0:T(8,128)} %param.16, f32[]{:T(128)} %constant.298.clone.1), padding=1_1x1_1x1_1x0_0x0_0x0_0 | pad | bytes 14680068 | tf_op jit(solution)/shard_map/scatter | solution.py:18
  24.3 0.0 copy-done.1
  24.3 0.6 gather_fusion
  24.8 0.0 collective-permute-done
  24.8 0.0 copy-done
  24.8 1.9 %collective-permute-start.5 = (f32[1,1,1,8,128,128]{5,4,3,2,1,0:T(8,128)S(1)}, f32[1,1,1,8,128,128]{5,4,3,2,1,0:T(8,128)S(1)}, u32[]{:S(2)}, u32[]{:S(2)}) collective-permute-start(f32[1,1,1,8,128,128]{5,4,3,2,1,0:T(8,128)S(1)} %copy-done), channel_id=1, source_target_pairs={{1,0},{2,1},{3,2},{5,4},{6,5},{7,6},{9,8},{10,9},{11,10},{13,12},{... | collective-permute-start | bytes 1572872 | tf_op jit(solution)/shard_map/ppermute | solution.py:12
  26.8 0.8 %constant_dynamic-update-slice_fusion.5 = f32[3,3,3,8,128,128]{5,4,3,2,1,0:T(8,128)} fusion(f32[3,3,3,8,128,128]{5,4,3,2,1,0:T(8,128)} %scatter.24, f32[1,1,1,8,128,128]{5,4,3,2,1,0:T(8,128)S(1)} %collective-permute-done), kind=kLoop, calls=%fused_computation.38 | loop fusion | bytes 1048576 | tf_op jit(solution)/shard_map/scatter | solution.py:19
  27.6 0.0 collective-permute-done.1
  27.6 0.8 %constant_dynamic-update-slice_fusion.4 = f32[3,3,3,8,128,128]{5,4,3,2,1,0:T(8,128)} fusion(f32[3,3,3,8,128,128]{5,4,3,2,1,0:T(8,128)} %constant_dynamic-update-slice_fusion.5, f32[1,1,1,8,128,128]{5,4,3,2,1,0:T(8,128)S(1)} %collective-permute-done.1), kind=kLoop, calls=%fused_computation.37 | loop fusion | bytes 1048576 | tf_op jit(solution)/shard_map/scatter | solution.py:20
  28.5 0.0 collective-permute-done.2
  28.5 0.9 %constant_dynamic-update-slice_fusion.3 = f32[3,3,3,8,128,128]{5,4,3,2,1,0:T(8,128)} fusion(f32[3,3,3,8,128,128]{5,4,3,2,1,0:T(8,128)} %constant_dynamic-update-slice_fusion.4, f32[1,1,1,8,128,128]{5,4,3,2,1,0:T(8,128)S(1)} %collective-permute-done.2), kind=kLoop, calls=%fused_computation.36 | loop fusion | bytes 1048576 | tf_op jit(solution)/shard_map/scatter | solution.py:21
  29.3 0.0 collective-permute-done.3
  29.3 0.9 %constant_dynamic-update-slice_fusion.2 = f32[3,3,3,8,128,128]{5,4,3,2,1,0:T(8,128)} fusion(f32[3,3,3,8,128,128]{5,4,3,2,1,0:T(8,128)} %constant_dynamic-update-slice_fusion.3, f32[1,1,1,8,128,128]{5,4,3,2,1,0:T(8,128)S(1)} %collective-permute-done.3), kind=kLoop, calls=%fused_computation.35 | loop fusion | bytes 1048576 | tf_op jit(solution)/shard_map/scatter | solution.py:22
  30.2 0.0 collective-permute-done.4
  30.2 0.8 %constant_dynamic-update-slice_fusion.1 = f32[3,3,3,8,128,128]{5,4,3,2,1,0:T(8,128)} fusion(f32[3,3,3,8,128,128]{5,4,3,2,1,0:T(8,128)} %constant_dynamic-update-slice_fusion.2, f32[1,1,1,8,128,128]{5,4,3,2,1,0:T(8,128)S(1)} %collective-permute-done.4), kind=kLoop, calls=%fused_computation.34 | loop fusion | bytes 1048576 | tf_op jit(solution)/shard_map/scatter | solution.py:23
  31.1 4.3 %collective-permute-done.5 = f32[1,1,1,8,128,128]{5,4,3,2,1,0:T(8,128)S(1)} collective-permute-done((f32[1,1,1,8,128,128]{5,4,3,2,1,0:T(8,128)S(1)}, f32[1,1,1,8,128,128]{5,4,3,2,1,0:T(8,128)S(1)}, u32[]{:S(2)}, u32[]{:S(2)}) %collective-permute-start.5) | collective-permute-done | bytes 524320 | tf_op jit(solution)/shard_map/ppermute | solution.py:12
  35.3 0.8 %constant_dynamic-update-slice_fusion = f32[3,3,3,8,128,128]{5,4,3,2,1,0:T(8,128)} fusion(f32[3,3,3,8,128,128]{5,4,3,2,1,0:T(8,128)} %constant_dynamic-update-slice_fusion.1, f32[1,1,1,8,128,128]{5,4,3,2,1,0:T(8,128)S(1)} %collective-permute-done.5), kind=kLoop, calls=%fused_computation.33 | loop fusion | bytes 1048576 | tf_op jit(solution)/shard_map/scatter | solution.py:24
  36.2 7.8 %gather_fusion.1 = f32[8,8,128,128]{3,2,1,0:T(8,128)} fusion(f32[27,8,128,128]{3,2,1,0:T(8,128)} %bitcast.90, s32[1024]{0:T(1024)S(1)} %pad_clamp_fusion), kind=kCustom, calls=%fused_computation.1 | custom fusion | bytes 8388640 | tf_op jit(solution)/shard_map/gather | solution.py:32
  44.0 8.3 %fusion = f32[8,8,128,128]{3,1,2,0:T(8,128)} fusion(f32[8,8,128,128]{3,2,1,0:T(8,128)} %gather_fusion.1, s32[8,8]{1,0:T(8,128)S(1)} %gather_fusion, s32[8]{0:T(128)S(1)} %bitcast.92, pred[8]{0:T(512)(128)(4,1)S(1)} %broadcast_compare_fusion, pred[8]{0:T(512)(128)(4,1)S(1)} %get-tuple-element.89), kind=kOutput, calls=%fused_computation.2 | convolution fusion | flops 100664832 | bytes 8388912 | tf_op jit(solution)/shard_map/tus,tuab->tsab/dot_general | solution.py:33
  52.3 5.3 %copy.8 = f32[8,8,128,128]{2,3,0,1:T(8,128)} copy(f32[8,8,128,128]{3,1,2,0:T(8,128)} %fusion) | data formatting | bytes 8388608 | tf_op jit(solution)/shard_map/tus,tuab->tsab/dot_general | solution.py:33
  57.6 5.2 %fusion.7 = f32[8,128,128,1]{2,1,3,0:T(8,128)S(1)} fusion(f32[8,8,128,128]{2,3,0,1:T(8,128)} %copy.8, f32[1,1,1,8,128,128]{5,4,3,2,1,0:T(8,128)S(1)} %copy-done), kind=kOutput, calls=%fused_computation.10 | convolution fusion | flops 1610612736 | bytes 5242880 | tf_op jit(solution)/shard_map/tab,tsbc->sac/dot_general | solution.py:35
  62.9 5.2 %fusion.5 = f32[1,1,1,8,128,128]{4,5,3,2,1,0:T(8,128)S(1)} fusion(f32[8,8,128,128]{2,3,0,1:T(8,128)} %copy.8, f32[8,128,128,1]{2,1,3,0:T(8,128)S(1)} %fusion.7), kind=kOutput, calls=%fused_computation.8 | convolution fusion | flops 1611005952 | bytes 5242880 | tf_op jit(solution)/shard_map/tab,tsbc->sac/dot_general | solution.py:36
  68.1 1.0 %copy.11 = f32[1,1,1,8,128,128]{5,4,3,2,1,0:T(8,128)} copy(f32[1,1,1,8,128,128]{4,5,3,2,1,0:T(8,128)S(1)} %fusion.5) | data formatting | bytes 1048576 | tf_op jit(solution)/shard_map/reshape;stack | solution.py:39
  (5 shorter events, 0.0 us)
Async XLA Ops:
  0.0 24.8 %copy-start = (f32[1,1,1,8,128,128]{5,4,3,2,1,0:T(8,128)S(1)}, f32[1,1,1,8,128,128]{5,4,3,2,1,0:T(8,128)}, u32[]{:S(2)}) copy-start(f32[1,1,1,8,128,128]{5,4,3,2,1,0:T(8,128)} %param.16) | copy-start | bytes 1572868
  0.0 24.3 %copy-start.1 = (s32[2,4,4,8]{3,2,1,0:T(4,128)S(1)}, s32[2,4,4,8]{3,2,1,0:T(4,128)}, u32[]{:S(2)}) copy-start(s32[2,4,4,8]{3,2,1,0:T(4,128)} %param.17) | copy-start | bytes 3076
  0.0 24.8 %collective-permute-start = (f32[1,1,1,8,128,128]{5,4,3,2,1,0:T(8,128)}, f32[1,1,1,8,128,128]{5,4,3,2,1,0:T(8,128)S(1)}, u32[]{:S(2)}, u32[]{:S(2)}) collective-permute-start(f32[1,1,1,8,128,128]{5,4,3,2,1,0:T(8,128)} %param.16), channel_id=1, source_target_pairs={{0,16},{1,17},{2,18},{3,19},{4,20},{5,21},{6,22},{7,23},{8,24},{9,... | collective-permute-start | bytes 1572872 | tf_op jit(solution)/shard_map/ppermute | solution.py:12
  1.4 26.2 %collective-permute-start.1 = (f32[1,1,1,8,128,128]{5,4,3,2,1,0:T(8,128)}, f32[1,1,1,8,128,128]{5,4,3,2,1,0:T(8,128)S(1)}, u32[]{:S(2)}, u32[]{:S(2)}) collective-permute-start(f32[1,1,1,8,128,128]{5,4,3,2,1,0:T(8,128)} %param.16), channel_id=1, source_target_pairs={{16,0},{17,1},{18,2},{19,3},{20,4},{21,5},{22,6},{23,7},{24,8},{25... | collective-permute-start | bytes 1572872 | tf_op jit(solution)/shard_map/ppermute | solution.py:12
  5.5 23.0 %collective-permute-start.2 = (f32[1,1,1,8,128,128]{5,4,3,2,1,0:T(8,128)}, f32[1,1,1,8,128,128]{5,4,3,2,1,0:T(8,128)S(1)}, u32[]{:S(2)}, u32[]{:S(2)}) collective-permute-start(f32[1,1,1,8,128,128]{5,4,3,2,1,0:T(8,128)} %param.16), channel_id=1, source_target_pairs={{0,4},{4,8},{8,12},{1,5},{5,9},{9,13},{2,6},{6,10},{10,14},{3,7},{... | collective-permute-start | bytes 1572872 | tf_op jit(solution)/shard_map/ppermute | solution.py:12
  6.8 22.6 %collective-permute-start.3 = (f32[1,1,1,8,128,128]{5,4,3,2,1,0:T(8,128)}, f32[1,1,1,8,128,128]{5,4,3,2,1,0:T(8,128)S(1)}, u32[]{:S(2)}, u32[]{:S(2)}) collective-permute-start(f32[1,1,1,8,128,128]{5,4,3,2,1,0:T(8,128)} %param.16), channel_id=1, source_target_pairs={{4,0},{8,4},{12,8},{5,1},{9,5},{13,9},{6,2},{10,6},{14,10},{7,3},{... | collective-permute-start | bytes 1572872 | tf_op jit(solution)/shard_map/ppermute | solution.py:12
  10.8 19.4 %collective-permute-start.4 = (f32[1,1,1,8,128,128]{5,4,3,2,1,0:T(8,128)}, f32[1,1,1,8,128,128]{5,4,3,2,1,0:T(8,128)S(1)}, u32[]{:S(2)}, u32[]{:S(2)}) collective-permute-start(f32[1,1,1,8,128,128]{5,4,3,2,1,0:T(8,128)} %param.16), channel_id=1, source_target_pairs={{0,1},{1,2},{2,3},{4,5},{5,6},{6,7},{8,9},{9,10},{10,11},{12,13},{... | collective-permute-start | bytes 1572872 | tf_op jit(solution)/shard_map/ppermute | solution.py:12
  24.8 10.5 %collective-permute-start.5 = (f32[1,1,1,8,128,128]{5,4,3,2,1,0:T(8,128)S(1)}, f32[1,1,1,8,128,128]{5,4,3,2,1,0:T(8,128)S(1)}, u32[]{:S(2)}, u32[]{:S(2)}) collective-permute-start(f32[1,1,1,8,128,128]{5,4,3,2,1,0:T(8,128)S(1)} %copy-done), channel_id=1, source_target_pairs={{1,0},{2,1},{3,2},{5,4},{6,5},{7,6},{9,8},{10,9},{11,10},{13,12},{... | collective-permute-start | bytes 1572872 | tf_op jit(solution)/shard_map/ppermute | solution.py:12
where the time goes:
time: 69.5 us; the launch traced here: 69.1 us
  local copies, waits for them, and re-layouts  27.6 us (40%)
  matrix products  18.8 us (27%)
  starting transfers between devices  17.5 us (25%)
  waiting for transfers between devices  4.31 us (6%)
  other arithmetic  0.74 us (1%)
    ppermute x6, starting transfers between devices, shifted(): lax.ppermute(value, axis, [(source, source + steps) for source in range(l...  17.5 us
    dot_general x1, matrix products, purify(): jnp.einsum('tus,tuab->tsab', matches[0], far_rows, precision=exact_mode)  8.33 us
    scatter x1, local copies, waits for them, and re-layouts, extend(): padded = padded.at[1:span_x + 1, 1:span_y + 1, 1:span_z + 1].set(current)  7.86 us
    gather x1, local copies, waits for them, and re-layouts, purify(): far_rows = padded[slot_index[0]]  7.78 us
    dot_general x1, local copies, waits for them, and re-layouts, purify(): jnp.einsum('tus,tuab->tsab', matches[0], far_rows, precision=exact_mode)  5.34 us
    dot_general x1, matrix products, purify(): cubed = jnp.einsum('tab,tsbc->sac', square, picked, precision=exact_mode)  5.24 us
    dot_general x1, matrix products, purify(): jnp.einsum('tab,tsbc->sac', row_blocks, picked, precision=exact_mode)  5.24 us
    ppermute x6, waiting for transfers between devices, shifted(): lax.ppermute(value, axis, [(source, source + steps) for source in range(l...  4.31 us
  transfers between devices with their start and end apart: 6, of which 1 were waited for; matrix products, arithmetic and copies ran while one was open for 19% of the time, Pallas kernels for 0%

commit v1 on v0

v1 whole, which is shorter than its diff:
```python
import functools

import jax
import jax.numpy as jnp
from jax import lax
from jax.experimental import pallas as pl
from jax.experimental.pallas import tpu as pltpu
from jax.sharding import PartitionSpec as P

MESH = pl.DeviceIdType.MESH
AXES = ("gx", "gy", "gz")


def directions(sizes):
    found = []
    for axis, size in enumerate(sizes):
        if size == 2:
            found.append((axis, 0))
        elif size > 2:
            found.extend([(axis, -1), (axis, 1)])
    return found


def split(value):
    head = value.astype(jnp.bfloat16)
    tail = (value - head.astype(jnp.float32)).astype(jnp.bfloat16)
    return jnp.concatenate([head, tail], axis=1)


def product(left, right):
    width = right.shape[1] // 2
    both = jnp.dot(left, jnp.concatenate([right, right], axis=0), preferred_element_type=jnp.float32)
    return both[:, :width] + both[:, width:]


def kernel(
    sizes, cols, blocks, out,
    own, far_diag, far_edge, edge, half, acc, res, shown,
    load_sem, send_d, recv_d, send_e, recv_e, store_sem,
):
    dirs = directions(sizes)
    count = len(dirs)
    kslots, block_size = own.shape[0], own.shape[1]
    where_am_i = [lax.axis_index(name) for name in AXES]
    strides = (sizes[1] * sizes[2], sizes[2], 1)
    me = sum(place * stride for place, stride in zip(where_am_i, strides))

    def opposite(d):
        axis, step = dirs[d]
        return dirs.index((axis, -step))

    def target(d):
        axis, step = dirs[d]
        place = where_am_i[axis]
        return (1 - place) if step == 0 else place + step

    def neighbour_id(d):
        axis, _ = dirs[d]
        return me + (target(d) - where_am_i[axis]) * strides[axis]

    def exists(d):
        axis, step = dirs[d]
        if step == 0:
            return None
        place = where_am_i[axis]
        return place > 0 if step < 0 else place < sizes[axis] - 1

    def if_exists(d, action):
        there = exists(d)
        if there is None:
            action()
        else:
            pl.when(there)(action)

    def send(d, src, dst, send_sem, recv_sem):
        return pltpu.make_async_remote_copy(
            src_ref=src,
            dst_ref=dst.at[opposite(d)],
            send_sem=send_sem.at[d],
            recv_sem=recv_sem.at[opposite(d)],
            device_id={AXES[dirs[d][0]]: target(d)},
            device_id_type=MESH,
        )

    def arrival(d, src, dst, send_sem, recv_sem):
        return pltpu.make_async_remote_copy(
            src_ref=src,
            dst_ref=dst.at[d],
            send_sem=send_sem.at[d],
            recv_sem=recv_sem.at[d],
            device_id={AXES[dirs[d][0]]: target(d)},
            device_id_type=MESH,
        )

    load = pltpu.make_async_copy(blocks, own, load_sem)
    load.start()
    barrier = pltpu.get_barrier_semaphore()
    for d in range(count):
        if_exists(
            d,
            lambda d=d: pl.semaphore_signal(
                barrier, inc=1, device_id={AXES[dirs[d][0]]: target(d)}, device_id_type=MESH
            ),
        )
    for d in range(count):
        there = exists(d)
        if there is not None:

            @pl.when(jnp.logical_not(there))
            def _(d=d):
                far_diag[d] = jnp.zeros((block_size, block_size), jnp.float32)
                far_edge[d] = jnp.zeros((block_size, block_size), jnp.float32)

    named = [cols[where_am_i[0], where_am_i[1], where_am_i[2], s] for s in range(kslots)]
    matches = [[named[s] == neighbour_id(d) for s in range(1, kslots)] for d in range(count)]
    load.wait()
    for d in range(count):
        total = jnp.where(matches[d][0], own[1], 0.0)
        for s in range(2, kslots):
            total = total + jnp.where(matches[d][s - 1], own[s], 0.0)
        edge[d] = total
    peers = jnp.int32(0)
    for d in range(count):
        there = exists(d)
        peers = peers + (1 if there is None else there.astype(jnp.int32))
    pl.semaphore_wait(barrier, peers)
    for d in range(count):
        if_exists(d, lambda d=d: send(d, edge.at[d], far_edge, send_e, recv_e).start())
    for d in range(count):
        if_exists(d, lambda d=d: send(d, own.at[0], far_diag, send_d, recv_d).start())

    half[0] = split(own[0])
    for d in range(count):
        half[1 + d] = split(edge[d])
    for d in range(count):
        acc[d] = product(half[0], half[1 + d])
    square = product(half[0], half[0])
    order = list(range(count))[::-1]
    for d in order:
        if_exists(d, lambda d=d: arrival(d, edge.at[d], far_edge, send_e, recv_e).wait_recv())
        arrived = split(far_edge[d])
        half[1 + count + d] = arrived
        square = square + product(half[1 + d], arrived)
    own_square = split(square)
    cubed = product(own_square, half[0])
    for d in range(count):
        res[1 + d] = product(own_square, half[1 + d])
    for d in order:
        if_exists(d, lambda d=d: arrival(d, own.at[0], far_diag, send_d, recv_d).wait_recv())
        arrived = split(far_diag[d])
        near = acc[d] + product(half[1 + d], arrived)
        repeats = sum(match.astype(jnp.int32) for match in matches[d]).astype(jnp.float32)
        weighted = split(near * repeats)
        res[1 + d] = 3.0 * near - 2.0 * (res[1 + d] + product(weighted, arrived))
        cubed = cubed + product(weighted, half[1 + count + d])
    res[0] = jnp.zeros((block_size, block_size), jnp.float32)
    shown[0] = 3.0 * square - 2.0 * cubed
    pltpu.make_async_copy(shown.at[0], out.at[0], store_sem.at[0]).start()
    for s in range(1, kslots):
        index = jnp.int32(0)
        for d in range(count):
            index = jnp.where(matches[d][s - 1], 1 + d, index)
        shown[s] = res[index]
        pltpu.make_async_copy(shown.at[s], out.at[s], store_sem.at[s]).start()
    for s in range(kslots):
        pltpu.make_async_copy(shown.at[s], out.at[s], store_sem.at[s]).wait()
    for d in range(count):
        if_exists(d, lambda d=d: send(d, edge.at[d], far_edge, send_e, recv_e).wait_send())
        if_exists(d, lambda d=d: send(d, own.at[0], far_diag, send_d, recv_d).wait_send())


def on_device(sizes, blocks, columns):
    kslots, block_size = blocks.shape[3], blocks.shape[4]
    count = len(directions(sizes))
    block = (block_size, block_size)
    renewed = pl.pallas_call(
        functools.partial(kernel, sizes),
        out_shape=jax.ShapeDtypeStruct((kslots,) + block, jnp.float32),
        in_specs=[
            pl.BlockSpec(memory_space=pltpu.SMEM),
            pl.BlockSpec(memory_space=pl.ANY),
        ],
        out_specs=pl.BlockSpec(memory_space=pl.ANY),
        scratch_shapes=[
            pltpu.VMEM((kslots,) + block, jnp.float32),
            pltpu.VMEM((count,) + block, jnp.float32),
            pltpu.VMEM((count,) + block, jnp.float32),
            pltpu.VMEM((count,) + block, jnp.float32),
            pltpu.VMEM((1 + 2 * count, block_size, 2 * block_size), jnp.bfloat16),
            pltpu.VMEM((count,) + block, jnp.float32),
            pltpu.VMEM((1 + count,) + block, jnp.float32),
            pltpu.VMEM((kslots,) + block, jnp.float32),
            pltpu.SemaphoreType.DMA,
            pltpu.SemaphoreType.DMA((count,)),
            pltpu.SemaphoreType.DMA((count,)),
            pltpu.SemaphoreType.DMA((count,)),
            pltpu.SemaphoreType.DMA((count,)),
            pltpu.SemaphoreType.DMA((kslots,)),
        ],
        compiler_params=pltpu.CompilerParams(
            collective_id=0, has_side_effects=True, vmem_limit_bytes=8 * 1024 * 1024
        ),
    )(columns, blocks.reshape((kslots,) + block))
    return renewed.reshape(blocks.shape)


def solution(mesh):
    sizes = tuple(mesh.shape[name] for name in AXES)
    return jax.shard_map(
        functools.partial(on_device, sizes),
        mesh=mesh,
        in_specs=(P("gx", "gy", "gz", None, None, None), P()),
        out_specs=P("gx", "gy", "gz", None, None, None),
        check_vma=False,
    )
```

time: 69.5 us -> 14.8 us (0.21)
  the two profiles are of different devices: /device:TPU:29 before, /device:TPU:0 now
where the time goes in v1:
time: 14.8 us; the launch traced here: 14.5 us
  Pallas kernels  12 us (81%)
  local copies, waits for them, and re-layouts  2.55 us (17%)
    pallas_call x1, Pallas kernels, on_device(): pl.pallas_call(functools.partial(kernel, sizes), out_shape=jax.ShapeDtype...  12 us
    unnamed x5, local copies, waits for them, and re-layouts  2.55 us

profile of v1, /device:TPU:0, one launch (start us, length us, event | category | flops | bytes accessed | tf_op | source)
XLA Modules:
  0.0 14.5 jit_solution(13952658320980859092)
XLA Ops:
  0.0 0.0 copy-start
  0.0 1.0 %copy-done = f32[1,1,1,8,128,128]{5,4,3,2,1,0:T(8,128)S(1)} copy-done((f32[1,1,1,8,128,128]{5,4,3,2,1,0:T(8,128)S(1)}, f32[1,1,1,8,128,128]{5,4,3,2,1,0:T(8,128)}, u32[]{:S(2)}) %copy-start) | copy-done | bytes 524312
  1.0 0.0 copy-start.1
  1.0 0.7 %copy-done.1 = s32[2,4,4,8]{3,2,1,0:T(4,128)S(1)} copy-done((s32[2,4,4,8]{3,2,1,0:T(4,128)S(1)}, s32[2,4,4,8]{3,2,1,0:T(4,128)}, u32[]{:S(2)}) %copy-start.1) | copy-done | bytes 1048
  1.8 12.0 %shard_map.28 = f32[8,128,128]{2,1,0:T(8,128)S(1)} custom-call(s32[2,4,4,8]{3,2,1,0:T(4,128)S(1)} %copy-done.1, f32[8,128,128]{2,1,0:T(8,128)S(1)} %bitcast.3), custom_call_target="tpu_custom_call" | custom-call | tf_op jit(solution)/shard_map/pallas_call | solution.py:176
  13.7 0.8 %copy.4 = f32[1,1,1,8,128,128]{5,4,3,2,1,0:T(8,128)} copy(f32[1,1,1,8,128,128]{5,4,3,2,1,0:T(8,128)S(1)} %bitcast.2) | data formatting | bytes 1048576
Async XLA Ops:
  0.0 1.0 %copy-start = (f32[1,1,1,8,128,128]{5,4,3,2,1,0:T(8,128)S(1)}, f32[1,1,1,8,128,128]{5,4,3,2,1,0:T(8,128)}, u32[]{:S(2)}) copy-start(f32[1,1,1,8,128,128]{5,4,3,2,1,0:T(8,128)} %param.2) | copy-start | bytes 1572868
  1.0 0.7 %copy-start.1 = (s32[2,4,4,8]{3,2,1,0:T(4,128)S(1)}, s32[2,4,4,8]{3,2,1,0:T(4,128)}, u32[]{:S(2)}) copy-start(s32[2,4,4,8]{3,2,1,0:T(4,128)} %cols.1) | copy-start | bytes 3076
